TPU v7x, 32 devices: a whole 2x2x4 slice. The times are simulated.
32 devices in a mesh: prow: 8 (over z, y), pcol: 4 (over x, core).
Axes of the slice: x: 2, y: 2, z: 4, core: 2. Of those that a mesh axis runs over, the one named last changes fastest.
Arguments:
- paper_x: bfloat16 [8192, 768], P(('prow', 'pcol')), may hold values from -6 to 6
- author_x: bfloat16 [4096, 768], P(('pcol', 'prow')), may hold values from -6 to 6
- w_self: bfloat16 [768, 768], replicated, may hold values from -0.21875 to 0.21875
- w_rel: bfloat16 [2, 768, 768], replicated, may hold values from -0.009765625 to 0.009765625
- w_two: bfloat16 [768, 768], replicated, may hold values from -0.0068359375 to 0.0068359375
- block_rows: int32 [8, 4, 32], P('prow', 'pcol'), may hold values from 0 to 7, as said below
- block_cols: int32 [8, 4, 32], P('prow', 'pcol'), may hold values from 0 to 7, as said below
- block_type: int32 [8, 4, 32], P('prow', 'pcol'), may hold values from 0 to 1
- block_count: int32 [8, 4], P('prow', 'pcol'), may hold values from 8 to 32, as said below
- block_vals: bfloat16 [8, 4, 32, 128, 128], P('prow', 'pcol'), may hold values from 0 to 1, as said below
Outputs:
- paper_hidden: bfloat16 [8192, 768], P(('prow', 'pcol'))
- author_out: bfloat16 [4096, 768], P(('pcol', 'prow'))
Inputs may be any that keep to these rules, and one draw needn't show every extreme that they name: `block_rows`: within one tile the live and dead slots name distinct positions; block rows are below 8. `block_cols`: block columns are below 8; with block_rows, positions of one tile are distinct. `block_count`: slots 0 to count - 1 of a tile are live; some tile holds 32 live slots and some tile 32 // 4 in every draw. `block_vals`: every entry is 0 or 1.
All inputs are finite; a program needn't handle non-finite values.
Results may differ from a plain program's by a relative error of at most 0.0041.
Values may be sent and summed in bfloat16 or wider, within the bound.
A program may use at most 64 MiB of HBM per device.

v0:
```python
import jax
import jax.numpy as jnp
from jax import lax
from jax.sharding import PartitionSpec as P

GROUP = 16


def per_device(
    paper_x,
    author_x,
    w_self,
    w_rel,
    w_two,
    block_rows,
    block_cols,
    block_type,
    block_count,
    block_vals,
):
    slots = block_rows.shape[2]
    side = block_vals.shape[3]
    width = paper_x.shape[1]
    relations = w_rel.shape[0]
    groups = slots // GROUP
    own_rows = paper_x.shape[0]
    row_ids = block_rows.reshape(groups, GROUP)
    col_ids = block_cols.reshape(groups, GROUP)
    type_ids = block_type.reshape(groups, GROUP)
    live = (
        (jnp.arange(slots, dtype=jnp.int32) < block_count.reshape(()))
        .astype(jnp.float32)
        .reshape(groups, GROUP)
    )
    contents = block_vals.reshape(groups, GROUP, side, side)
    self_term = jnp.dot(paper_x, w_self, preferred_element_type=jnp.float32)
    authors = lax.all_gather(author_x, "prow", axis=0, tiled=True)
    messages = jnp.stack(
        [
            jnp.dot(authors, w_rel[index], preferred_element_type=jnp.float32)
            for index in range(relations)
        ]
    ).astype(jnp.bfloat16)
    col_blocks = messages.shape[1] // side
    row_blocks = own_rows * lax.axis_size("pcol") // side
    table = messages.reshape(relations * col_blocks, side, width)
    row_range = jnp.arange(row_blocks, dtype=jnp.int32)
    col_range = jnp.arange(col_blocks, dtype=jnp.int32)

    def first_hop(total, item):
        rows_now, cols_now, types_now, mask_now, content_now = item
        picked = table[types_now * col_blocks + cols_now]
        product = jnp.einsum(
            "kpa,kaf->kpf", content_now, picked, preferred_element_type=jnp.float32
        )
        placing = (rows_now[:, None] == row_range[None, :]).astype(jnp.float32) * mask_now[:, None]
        return (
            total + jnp.einsum("kr,kpf->rpf", placing, product, precision=lax.Precision.HIGHEST),
            None,
        )

    start = jnp.zeros((row_blocks, side, width), jnp.float32)
    partial_value, _ = lax.scan(first_hop, start, (row_ids, col_ids, type_ids, live, contents))
    partial_value = partial_value.reshape(row_blocks * side, width)
    summed = lax.psum_scatter(partial_value, "pcol", scatter_dimension=0, tiled=True)
    paper_hidden = jnp.maximum(self_term + summed, 0.0).astype(jnp.bfloat16)
    outgoing = jnp.dot(paper_hidden, w_two, preferred_element_type=jnp.float32).astype(jnp.bfloat16)
    paper_rows = lax.all_gather(outgoing, "pcol", axis=0, tiled=True).reshape(
        row_blocks, side, width
    )

    def second_hop(total, item):
        rows_now, cols_now, mask_now, content_now = item
        picked = paper_rows[rows_now]
        product = jnp.einsum(
            "kpa,kpf->kaf", content_now, picked, preferred_element_type=jnp.float32
        )
        placing = (cols_now[:, None] == col_range[None, :]).astype(jnp.float32) * mask_now[:, None]
        return (
            total + jnp.einsum("kc,kaf->caf", placing, product, precision=lax.Precision.HIGHEST),
            None,
        )

    start_two = jnp.zeros((col_blocks, side, width), jnp.float32)
    author_part, _ = lax.scan(second_hop, start_two, (row_ids, col_ids, live, contents))
    author_total = lax.psum_scatter(
        author_part.reshape(col_blocks * side, width), "prow", scatter_dimension=0, tiled=True
    )
    return (paper_hidden, author_total.astype(jnp.bfloat16))


def solution(mesh):
    return jax.shard_map(
        per_device,
        mesh=mesh,
        in_specs=(
            P(("prow", "pcol"), None),
            P(("pcol", "prow"), None),
            P(),
            P(),
            P(),
            P("prow", "pcol", None),
            P("prow", "pcol", None),
            P("prow", "pcol", None),
            P("prow", "pcol"),
            P("prow", "pcol", None, None, None),
        ),
        out_specs=(P(("prow", "pcol"), None), P(("pcol", "prow"), None)),
        check_vma=False,
    )
```

profile of v0, /device:TPU:0, one launch (start us, length us, event | category | flops | bytes accessed | tf_op | source)
XLA Modules:
  0.0 299.5 jit_solution(3397042512454895330)
XLA Ops:
  7.2 0.0 copy-start
  7.2 0.0 all-gather.3.cloned.1.call-start
  7.2 0.7 all-gather.3.cloned.1.call-update
  7.9 0.0 reduce-scatter.3.cloned.1.call-start
  8.0 0.5 broadcast.116
  8.5 1.3 reduce.9
  9.8 0.1 reshape.103
  9.9 1.3 reduce.11
  11.2 0.1 reshape.107
  11.3 1.3 reduce.10
  12.6 0.1 reshape.106
  13.4 43.8 %all-gather.3.cloned.1.call-done = bf16[1024,768]{1,0:T(8,128)(2,1)} async-done(((bf16[128,768]{1,0:T(8,128)(2,1)}), bf16[1024,768]{1,0:T(8,128)(2,1)}) %all-gather.3.cloned.1.call-update) | async-done | bytes 1572880 | tf_op jit(solution)/shard_map/all_gather | solution.py:37
  57.1 0.0 copy-start.4
  57.1 0.0 copy-start.5
  57.1 3.3 %fusion.41 = bf16[1,1024,768]{2,1,0:T(8,128)(2,1)S(1)} fusion(bf16[1024,768]{1,0:T(8,128)(2,1)} %all-gather.3.cloned.1.call-done, bf16[2,768,768]{2,1,0:T(8,128)(2,1)} %param.17), kind=kOutput, calls=%fused_computation.55 | convolution fusion | flops 1208745984 | bytes 4325376 | tf_op jit(solution)/shard_map/dot_general | solution.py:40
  60.4 0.0 copy-done.4
  60.4 0.0 copy-done.5
  60.4 1.4 fusion.42
  61.8 0.0 copy-start.1
  61.8 2.0 pad_maximum_fusion
  63.8 0.0 copy-done.1
  63.8 41.9 %while.22 = (s32[]{:T(128)}, f32[8,128,768]{2,0,1:T(8,128)}, s32[2,16]{1,0:T(2,128)S(1)}, f32[2,16]{1,0:T(2,128)S(1)}, bf16[2,16,128,128]{3,2,1,0:T(8,128)(2,1)S...) while((s32[]{:T(128)}, f32[8,128,768]{2,0,1:T(8,128)}, ...), condition=%wide.region_1.2_spmd.clone, body=%wide.region_0.1_spmd.clone.sunk | while | flops 555222400 | bytes 28840768 | solution.py:63
  63.8 4.3 %gather_fusion = bf16[16,128,768]{2,1,0:T(8,128)(2,1)} fusion(bf16[16,128,768]{2,1,0:T(8,128)(2,1)} %get-tuple-element.297, s32[1024]{0:T(1024)S(1)} %pad_clamp_fusion.4), kind=kCustom, calls=%fused_computation.clone.clone.1 | custom fusion | bytes 6291520 | tf_op jit(solution)/shard_map/while/body/eval_jaxpr/gather | solution.py:52
  68.1 5.5 %fusion.78 = f32[16,128,768]{2,1,0:T(8,128)} fusion(bf16[16,128,768]{2,1,0:T(8,128)(2,1)} %gather_fusion, bf16[2,16,128,128]{3,2,1,0:T(8,128)(2,1)S(1)} %get-tuple-element.294, s32[]{:T(128)} %get-tuple-element.280), kind=kOutput, calls=%fused_computation.7.clone.1 | convolution fusion | flops 402653184 | bytes 9961476 | tf_op jit(solution)/shard_map/while/body/eval_jaxpr/kpa,kaf->kpf/dot_general | solution.py:53
  73.6 10.9 %select_add_fusion.4 = f32[8,128,768]{2,0,1:T(8,128)} fusion(f32[8,128,768]{2,0,1:T(8,128)} %get-tuple-element.281, f32[16,128,768]{2,1,0:T(8,128)} %fusion.78, pred[]{:T(512)S(6)} %compare.6, f32[16]{0:T(128)S(1)} %fusion.79, s32[16]{0:T(128)S(1)} %fusion.80), kind=kOutput, calls=%fused_computation.6.clone.1 | convolution fusion | flops 152568064 | bytes 12583041 | tf_op jit(solution)/shard_map/while/body/eval_jaxpr/kr,kpf->rpf/dot_general | solution.py:58
  84.5 4.3 %gather_fusion = bf16[16,128,768]{2,1,0:T(8,128)(2,1)} fusion(bf16[16,128,768]{2,1,0:T(8,128)(2,1)} %get-tuple-element.297, s32[1024]{0:T(1024)S(1)} %pad_clamp_fusion.4), kind=kCustom, calls=%fused_computation.clone.clone.1 | custom fusion | bytes 6291520 | tf_op jit(solution)/shard_map/while/body/eval_jaxpr/gather | solution.py:52
  88.8 5.5 %fusion.78 = f32[16,128,768]{2,1,0:T(8,128)} fusion(bf16[16,128,768]{2,1,0:T(8,128)(2,1)} %gather_fusion, bf16[2,16,128,128]{3,2,1,0:T(8,128)(2,1)S(1)} %get-tuple-element.294, s32[]{:T(128)} %get-tuple-element.280), kind=kOutput, calls=%fused_computation.7.clone.1 | convolution fusion | flops 402653184 | bytes 9961476 | tf_op jit(solution)/shard_map/while/body/eval_jaxpr/kpa,kaf->kpf/dot_general | solution.py:53
  94.3 11.4 %select_add_fusion.4 = f32[8,128,768]{2,0,1:T(8,128)} fusion(f32[8,128,768]{2,0,1:T(8,128)} %get-tuple-element.281, f32[16,128,768]{2,1,0:T(8,128)} %fusion.78, pred[]{:T(512)S(6)} %compare.6, f32[16]{0:T(128)S(1)} %fusion.79, s32[16]{0:T(128)S(1)} %fusion.80), kind=kOutput, calls=%fused_computation.6.clone.1 | convolution fusion | flops 152568064 | bytes 12583041 | tf_op jit(solution)/shard_map/while/body/eval_jaxpr/kr,kpf->rpf/dot_general | solution.py:58
  105.7 4.6 %copy.12 = f32[8,128,768]{2,1,0:T(8,128)} copy(f32[8,128,768]{2,0,1:T(8,128)} %get-tuple-element.91) | data formatting | bytes 6291456 | tf_op jit(solution)/shard_map/while | solution.py:63
  110.3 0.0 copy-start.3
  110.3 0.0 reduce-scatter.3.cloned.1.call-update
  110.3 0.0 all-gather.5.cloned.1.call-start
  110.3 36.3 %reduce-scatter.3.cloned.1.call-done = f32[256,768]{1,0:T(8,128)} async-done(((f32[1024,768]{1,0:T(8,128)}), f32[256,768]{1,0:T(8,128)}) %reduce-scatter.3.cloned.1.call-update) | async-done | bytes 786448 | tf_op jit(solution)/shard_map/reduce_scatter | solution.py:65
  146.7 0.0 copy-done
  146.7 0.0 copy-done.3
  146.7 1.6 fusion.44
  148.3 0.0 copy-start.2
  148.3 2.6 convolution_convert_fusion.2
  151.0 0.0 all-gather.5.cloned.1.call-update
  151.0 0.2 reduce-scatter.5.cloned.1.call-start
  151.2 19.5 %all-gather.5.cloned.1.call-done = bf16[1024,768]{1,0:T(8,128)(2,1)} async-done(((bf16[256,768]{1,0:T(8,128)(2,1)}), bf16[1024,768]{1,0:T(8,128)(2,1)}) %all-gather.5.cloned.1.call-update) | async-done | bytes 1572880 | tf_op jit(solution)/shard_map/all_gather | solution.py:68
  170.8 0.0 copy-done.2
  170.8 41.2 %while.23 = (s32[]{:T(128)}, f32[8,128,768]{2,0,1:T(8,128)}, s32[2,16]{1,0:T(2,128)S(1)}, f32[2,16]{1,0:T(2,128)S(1)}, bf16[2,16,128,128]{3,2,1,0:T(8,128)(2,1)S...) while((s32[]{:T(128)}, f32[8,128,768]{2,0,1:T(8,128)}, ...), condition=%wide.region_4.5_spmd.clone, body=%wide.region_3.4_spmd.clone.sunk | while | flops 555222336 | bytes 28840696 | solution.py:85
  170.8 3.8 %gather_fusion.1 = bf16[16,128,768]{2,1,0:T(8,128)(2,1)} fusion(bf16[8,128,768]{2,1,0:T(8,128)(2,1)} %get-tuple-element.324, s32[1024]{0:T(1024)S(1)} %pad_clamp_fusion.5), kind=kCustom, calls=%fused_computation.1.clone.clone.1 | custom fusion | bytes 6291520 | tf_op jit(solution)/shard_map/while/body/eval_jaxpr/gather | solution.py:74
  174.6 5.6 %fusion.86 = f32[16,128,768]{2,1,0:T(8,128)} fusion(bf16[16,128,768]{2,1,0:T(8,128)(2,1)} %gather_fusion.1, bf16[2,16,128,128]{3,2,1,0:T(8,128)(2,1)S(1)} %get-tuple-element.322, s32[]{:T(128)} %get-tuple-element.309), kind=kOutput, calls=%fused_computation.32.clone.1 | convolution fusion | flops 402653184 | bytes 9961476 | tf_op jit(solution)/shard_map/while/body/eval_jaxpr/kpa,kpf->kaf/dot_general | solution.py:75
  180.2 11.0 %select_add_fusion.5 = f32[8,128,768]{2,0,1:T(8,128)} fusion(f32[8,128,768]{2,0,1:T(8,128)} %get-tuple-element.310, f32[16,128,768]{2,1,0:T(8,128)} %fusion.86, pred[]{:T(512)S(6)} %compare.7, f32[16]{0:T(128)S(1)} %fusion.87, s32[16]{0:T(128)S(1)} %fusion.88), kind=kOutput, calls=%fused_computation.31.clone.1 | convolution fusion | flops 152568064 | bytes 12583041 | tf_op jit(solution)/shard_map/while/body/eval_jaxpr/kc,kaf->caf/dot_general | solution.py:80
  191.2 3.8 %gather_fusion.1 = bf16[16,128,768]{2,1,0:T(8,128)(2,1)} fusion(bf16[8,128,768]{2,1,0:T(8,128)(2,1)} %get-tuple-element.324, s32[1024]{0:T(1024)S(1)} %pad_clamp_fusion.5), kind=kCustom, calls=%fused_computation.1.clone.clone.1 | custom fusion | bytes 6291520 | tf_op jit(solution)/shard_map/while/body/eval_jaxpr/gather | solution.py:74
  195.0 5.6 %fusion.86 = f32[16,128,768]{2,1,0:T(8,128)} fusion(bf16[16,128,768]{2,1,0:T(8,128)(2,1)} %gather_fusion.1, bf16[2,16,128,128]{3,2,1,0:T(8,128)(2,1)S(1)} %get-tuple-element.322, s32[]{:T(128)} %get-tuple-element.309), kind=kOutput, calls=%fused_computation.32.clone.1 | convolution fusion | flops 402653184 | bytes 9961476 | tf_op jit(solution)/shard_map/while/body/eval_jaxpr/kpa,kpf->kaf/dot_general | solution.py:75
  200.5 11.4 %select_add_fusion.5 = f32[8,128,768]{2,0,1:T(8,128)} fusion(f32[8,128,768]{2,0,1:T(8,128)} %get-tuple-element.310, f32[16,128,768]{2,1,0:T(8,128)} %fusion.86, pred[]{:T(512)S(6)} %compare.7, f32[16]{0:T(128)S(1)} %fusion.87, s32[16]{0:T(128)S(1)} %fusion.88), kind=kOutput, calls=%fused_computation.31.clone.1 | convolution fusion | flops 152568064 | bytes 12583041 | tf_op jit(solution)/shard_map/while/body/eval_jaxpr/kc,kaf->caf/dot_general | solution.py:80
  212.0 4.6 %copy.13 = f32[8,128,768]{2,1,0:T(8,128)} copy(f32[8,128,768]{2,0,1:T(8,128)} %get-tuple-element.92) | data formatting | bytes 6291456 | tf_op jit(solution)/shard_map/while | solution.py:85
  216.5 0.0 reduce-scatter.5.cloned.1.call-update
  216.5 74.7 %reduce-scatter.5.cloned.1.call-done = f32[128,768]{1,0:T(8,128)} async-done(((f32[1024,768]{1,0:T(8,128)}), f32[128,768]{1,0:T(8,128)}) %reduce-scatter.5.cloned.1.call-update) | async-done | bytes 393232 | tf_op jit(solution)/shard_map/reduce_scatter | solution.py:86
  291.2 1.7 convert_element_type.24
  (19 shorter events, 0.1 us)
Async XLA Ops:
  7.2 139.5 %copy-start = (bf16[768,768]{1,0:T(8,128)(2,1)S(1)}, bf16[768,768]{1,0:T(8,128)(2,1)}, u32[]{:S(2)}) copy-start(bf16[768,768]{1,0:T(8,128)(2,1)} %param.16) | copy-start | bytes 3538948
  7.2 49.9 %all-gather.3.cloned.1.call-start = ((), (), s32[]{:S(2)}) async-start(), calls=%async_computation.2 | async-start | bytes 1769472 | tf_op jit(solution)/shard_map/all_gather | solution.py:37
  7.9 138.8 %reduce-scatter.3.cloned.1.call-start = ((), (), s32[]{:S(2)}) async-start(), calls=%async_computation.3 | async-start | bytes 3932160 | tf_op jit(solution)/shard_map/reduce_scatter | solution.py:65
  57.1 3.3 %copy-start.4 = (bf16[2,768,768]{2,1,0:T(8,128)(2,1)S(1)}, bf16[2,768,768]{2,1,0:T(8,128)(2,1)}, u32[]{:S(2)}) copy-start(bf16[2,768,768]{2,1,0:T(8,128)(2,1)} %param.17) | copy-start | bytes 7077892
  57.1 3.3 %copy-start.5 = (bf16[1024,768]{1,0:T(8,128)(2,1)S(1)}, bf16[1024,768]{1,0:T(8,128)(2,1)}, u32[]{:S(2)}) copy-start(bf16[1024,768]{1,0:T(8,128)(2,1)} %all-gather.3.cloned.1.call-done) | copy-start | bytes 4718596
  61.8 2.0 copy-start.1
  110.3 36.4 %copy-start.3 = (bf16[256,768]{1,0:T(8,128)(2,1)S(1)}, bf16[256,768]{1,0:T(8,128)(2,1)}, u32[]{:S(2)}) copy-start(bf16[256,768]{1,0:T(8,128)(2,1)} %param.14) | copy-start | bytes 1179652
  110.3 60.5 %all-gather.5.cloned.1.call-start = ((), (), s32[]{:S(2)}) async-start(), calls=%async_computation.4 | async-start | bytes 1966080 | tf_op jit(solution)/shard_map/all_gather | solution.py:68
  148.3 22.5 %copy-start.2 = (bf16[256,768]{1,0:T(8,128)(2,1)}, bf16[256,768]{1,0:T(8,128)(2,1)S(1)}, u32[]{:S(2)}) copy-start(bf16[256,768]{1,0:T(8,128)(2,1)S(1)} %fusion.44) | copy-start | bytes 1179652
  151.0 140.3 %reduce-scatter.5.cloned.1.call-start = ((), (), s32[]{:S(2)}) async-start(), calls=%async_computation.5 | async-start | bytes 3538944 | tf_op jit(solution)/shard_map/reduce_scatter | solution.py:86
Sparse Core Ops, SparseCore 0:
  10.2 46.8 all-gather.2
  110.4 36.2 reduce-scatter.2
  151.1 19.6 all-gather.4
  216.7 74.5 reduce-scatter.4
where the time goes:
time: 300 us; the launch traced here: 299 us
  waiting for transfers between devices  175 us (58%)
  matrix products  75.7 us (25%)
  local copies, waits for them, and re-layouts  26.1 us (9%)
  between operations  14.5 us (5%)
  other arithmetic  7.68 us (3%)
    reduce_scatter x1, waiting for transfers between devices, per_device(): lax.psum_scatter(author_part.reshape(col_blocks * side, width), 'prow', s...  74.7 us
    all_gather x1, waiting for transfers between devices, per_device(): authors = lax.all_gather(author_x, 'prow', axis=0, tiled=True)  43.8 us
    reduce_scatter x1, waiting for transfers between devices, per_device(): lax.psum_scatter(partial_value, 'pcol', scatter_dimension=0, tiled=True)  36.3 us
    dot_general x2, matrix products, second_hop(): jnp.einsum('kc,kaf->caf', placing, product, precision=lax.Precision.HIGHEST)  22.4 us
    dot_general x2, matrix products, first_hop(): jnp.einsum('kr,kpf->rpf', placing, product, precision=lax.Precision.HIGHEST)  22.3 us
    all_gather x1, waiting for transfers between devices, per_device(): lax.all_gather(outgoing, 'pcol', axis=0, tiled=True)  19.5 us
    dot_general x2, matrix products, second_hop(): jnp.einsum('kpa,kpf->kaf', content_now, picked, preferred_element_type=jn...  11.1 us
    dot_general x2, matrix products, first_hop(): jnp.einsum('kpa,kaf->kpf', content_now, picked, preferred_element_type=jn...  11 us
  transfers between devices with their start and end apart: 4, of which 4 were waited for; matrix products, arithmetic and copies ran while one was open for 2% of the time, Pallas kernels for 0%

commit v1 on v0

--- a/solution.py
+++ b/solution.py
@@ -4,6 +4,27 @@
 from jax.sharding import PartitionSpec as P
 
 GROUP = 16
+
+
+def ring_gather(x, axis, dim):
+    peers, index, extent = (lax.axis_size(axis), lax.axis_index(axis), x.shape[dim])
+    upward = [(i, (i + 1) % peers) for i in range(peers)]
+    downward = [(i, (i - 1) % peers) for i in range(peers)]
+    out = jnp.zeros((*x.shape[:dim], peers * extent, *x.shape[dim + 1 :]), x.dtype)
+    out = lax.dynamic_update_slice_in_dim(out, x, index * extent, axis=dim)
+    from_left = from_right = x
+    halfway = peers // 2
+    for step in range(1, halfway + 1):
+        from_left = lax.ppermute(from_left, axis, upward)
+        out = lax.dynamic_update_slice_in_dim(
+            out, from_left, (index - step) % peers * extent, axis=dim
+        )
+        if step < peers - halfway:
+            from_right = lax.ppermute(from_right, axis, downward)
+            out = lax.dynamic_update_slice_in_dim(
+                out, from_right, (index + step) % peers * extent, axis=dim
+            )
+    return out
 
 
 def per_device(
@@ -65,9 +86,7 @@
     summed = lax.psum_scatter(partial_value, "pcol", scatter_dimension=0, tiled=True)
     paper_hidden = jnp.maximum(self_term + summed, 0.0).astype(jnp.bfloat16)
     outgoing = jnp.dot(paper_hidden, w_two, preferred_element_type=jnp.float32).astype(jnp.bfloat16)
-    paper_rows = lax.all_gather(outgoing, "pcol", axis=0, tiled=True).reshape(
-        row_blocks, side, width
-    )
+    paper_rows = ring_gather(outgoing, "pcol", 0).reshape(row_blocks, side, width)
 
     def second_hop(total, item):
         rows_now, cols_now, mask_now, content_now = item

time: 300 us -> 295 us (0.983)
  waiting for transfers between devices: 175 us -> 170 us
    all_gather x1 -> x0, waiting for transfers between devices: 19.5 us -> none  [per_device(): lax.all_gather(outgoing, 'pcol', axis=0, tiled=True)]
    ppermute x0 -> x3, waiting for transfers between devices: none -> 14.6 us  [the longest x2 14.6 us: ring_gather(): from_left = lax.ppermute(from_left, axis, upward)]
    dynamic_update_slice x0 -> x3, local copies, waits for them, and re-layouts: none -> 3.08 us  [the longest x2 2.05 us: ring_gather(): lax.dynamic_update_slice_in_dim(out, from_left, (index - step) % peers *...]
  transfers between devices with their start and end apart: 4 -> 6, of which waited for: 4 -> 5; matrix products, arithmetic and copies ran while one was open for 2% -> 2% of each run, Pallas kernels for 0% -> 0%
where the time goes in v1:
time: 295 us
  waiting for transfers between devices  170 us (58%)
  matrix products  74.1 us (25%)
  local copies, waits for them, and re-layouts  26.5 us (9%)
  between operations  14.5 us (5%)
  other arithmetic  7.69 us (3%)
    reduce_scatter x1, waiting for transfers between devices, per_device(): lax.psum_scatter(author_part.reshape(col_blocks * side, width), 'prow', s...  74.4 us
    all_gather x1, waiting for transfers between devices, per_device(): authors = lax.all_gather(author_x, 'prow', axis=0, tiled=True)  43.8 us
    reduce_scatter x1, waiting for transfers between devices, per_device(): lax.psum_scatter(partial_value, 'pcol', scatter_dimension=0, tiled=True)  36.3 us
    dot_general x2, matrix products, first_hop(): jnp.einsum('kr,kpf->rpf', placing, product, precision=lax.Precision.HIGHEST)  22.4 us
    dot_general x2, matrix products, second_hop(): jnp.einsum('kc,kaf->caf', placing, product, precision=lax.Precision.HIGHEST)  22.4 us
    ppermute x2, waiting for transfers between devices, ring_gather(): from_left = lax.ppermute(from_left, axis, upward)  14.6 us
    dot_general x2, matrix products, second_hop(): jnp.einsum('kpa,kpf->kaf', content_now, picked, preferred_element_type=jn...  11.5 us
    dot_general x2, matrix products, first_hop(): jnp.einsum('kpa,kaf->kpf', content_now, picked, preferred_element_type=jn...  11 us
  transfers between devices with their start and end apart: 6, of which 5 were waited for; matrix products, arithmetic and copies ran while one was open for 2% of the time, Pallas kernels for 0%

profile of v1, /device:TPU:0, one launch (start us, length us, event | category | flops | bytes accessed | tf_op | source)
XLA Modules:
  0.0 294.5 jit_solution(13100173751352111013)
XLA Ops:
  7.2 0.0 copy-start
  7.2 0.0 all-gather.2.cloned.1.call-start
  7.2 0.7 all-gather.2.cloned.1.call-update
  7.9 0.0 reduce-scatter.3.cloned.1.call-start
  8.0 0.5 broadcast.119
  8.5 1.3 reduce.9
  9.8 0.1 reshape.103
  10.5 1.3 reduce.10
  11.9 0.1 reshape.106
  11.9 1.3 reduce.11
  13.3 0.1 reshape.107
  13.4 43.8 %all-gather.2.cloned.1.call-done = bf16[1024,768]{1,0:T(8,128)(2,1)} async-done(((bf16[128,768]{1,0:T(8,128)(2,1)}), bf16[1024,768]{1,0:T(8,128)(2,1)}) %all-gather.2.cloned.1.call-update) | async-done | bytes 1572880 | tf_op jit(solution)/shard_map/all_gather | solution.py:58
  57.1 0.0 copy-start.5
  57.1 0.0 copy-start.6
  57.1 3.3 %fusion.42 = bf16[1,1024,768]{2,1,0:T(8,128)(2,1)S(1)} fusion(bf16[1024,768]{1,0:T(8,128)(2,1)} %all-gather.2.cloned.1.call-done, bf16[2,768,768]{2,1,0:T(8,128)(2,1)} %param.17), kind=kOutput, calls=%fused_computation.56 | convolution fusion | flops 1208745984 | bytes 4325376 | tf_op jit(solution)/shard_map/dot_general | solution.py:61
  60.4 0.0 copy-done.5
  60.4 0.0 copy-done.6
  60.4 1.4 fusion.41
  61.8 0.0 copy-start.1
  61.8 2.0 pad_maximum_fusion
  63.8 0.0 copy-done.1
  63.8 42.1 %while.22 = (s32[]{:T(128)}, f32[8,128,768]{2,0,1:T(8,128)}, s32[2,16]{1,0:T(2,128)S(1)}, f32[2,16]{1,0:T(2,128)S(1)}, bf16[2,16,128,128]{3,2,1,0:T(8,128)(2,1)S...) while((s32[]{:T(128)}, f32[8,128,768]{2,0,1:T(8,128)}, ...), condition=%wide.region_1.2_spmd.clone, body=%wide.region_0.1_spmd.clone.sunk | while | flops 555222400 | bytes 28840776 | solution.py:84
  63.8 4.3 %gather_fusion = bf16[16,128,768]{2,1,0:T(8,128)(2,1)} fusion(bf16[16,128,768]{2,1,0:T(8,128)(2,1)} %get-tuple-element.299, s32[1024]{0:T(1024)S(1)} %pad_clamp_fusion.4), kind=kCustom, calls=%fused_computation.clone.clone.1 | custom fusion | bytes 6291520 | tf_op jit(solution)/shard_map/while/body/eval_jaxpr/gather | solution.py:73
  68.1 5.5 %fusion.78 = f32[16,128,768]{2,1,0:T(8,128)} fusion(bf16[16,128,768]{2,1,0:T(8,128)(2,1)} %gather_fusion, bf16[2,16,128,128]{3,2,1,0:T(8,128)(2,1)S(1)} %get-tuple-element.296, s32[]{:T(128)S(6)} %copy.30), kind=kOutput, calls=%fused_computation.7.clone.1 | convolution fusion | flops 402653184 | bytes 9961476 | tf_op jit(solution)/shard_map/while/body/eval_jaxpr/kpa,kaf->kpf/dot_general | solution.py:74
  73.6 11.0 %select_add_fusion.4 = f32[8,128,768]{2,0,1:T(8,128)} fusion(f32[8,128,768]{2,0,1:T(8,128)} %get-tuple-element.283, f32[16,128,768]{2,1,0:T(8,128)} %fusion.78, pred[]{:T(512)S(6)} %compare.9, f32[16]{0:T(128)S(1)} %fusion.79, s32[16]{0:T(128)S(1)} %fusion.80), kind=kOutput, calls=%fused_computation.6.clone.1 | convolution fusion | flops 152568064 | bytes 12583041 | tf_op jit(solution)/shard_map/while/body/eval_jaxpr/kr,kpf->rpf/dot_general | solution.py:79
  84.7 4.3 %gather_fusion = bf16[16,128,768]{2,1,0:T(8,128)(2,1)} fusion(bf16[16,128,768]{2,1,0:T(8,128)(2,1)} %get-tuple-element.299, s32[1024]{0:T(1024)S(1)} %pad_clamp_fusion.4), kind=kCustom, calls=%fused_computation.clone.clone.1 | custom fusion | bytes 6291520 | tf_op jit(solution)/shard_map/while/body/eval_jaxpr/gather | solution.py:73
  88.9 5.5 %fusion.78 = f32[16,128,768]{2,1,0:T(8,128)} fusion(bf16[16,128,768]{2,1,0:T(8,128)(2,1)} %gather_fusion, bf16[2,16,128,128]{3,2,1,0:T(8,128)(2,1)S(1)} %get-tuple-element.296, s32[]{:T(128)S(6)} %copy.30), kind=kOutput, calls=%fused_computation.7.clone.1 | convolution fusion | flops 402653184 | bytes 9961476 | tf_op jit(solution)/shard_map/while/body/eval_jaxpr/kpa,kaf->kpf/dot_general | solution.py:74
  94.5 11.5 %select_add_fusion.4 = f32[8,128,768]{2,0,1:T(8,128)} fusion(f32[8,128,768]{2,0,1:T(8,128)} %get-tuple-element.283, f32[16,128,768]{2,1,0:T(8,128)} %fusion.78, pred[]{:T(512)S(6)} %compare.9, f32[16]{0:T(128)S(1)} %fusion.79, s32[16]{0:T(128)S(1)} %fusion.80), kind=kOutput, calls=%fused_computation.6.clone.1 | convolution fusion | flops 152568064 | bytes 12583041 | tf_op jit(solution)/shard_map/while/body/eval_jaxpr/kr,kpf->rpf/dot_general | solution.py:79
  105.9 4.5 %copy.12 = f32[8,128,768]{2,1,0:T(8,128)} copy(f32[8,128,768]{2,0,1:T(8,128)} %get-tuple-element.91) | data formatting | bytes 6291456 | tf_op jit(solution)/shard_map/while | solution.py:84
  110.5 0.0 copy-start.3
  110.5 0.0 copy-start.4
  110.5 0.0 reduce-scatter.3.cloned.1.call-update
  110.5 0.0 reduce-scatter.5.cloned.1.call-start
  110.5 36.3 %reduce-scatter.3.cloned.1.call-done = f32[256,768]{1,0:T(8,128)} async-done(((f32[1024,768]{1,0:T(8,128)}), f32[256,768]{1,0:T(8,128)}) %reduce-scatter.3.cloned.1.call-update) | async-done | bytes 786448 | tf_op jit(solution)/shard_map/reduce_scatter | solution.py:86
  146.9 0.0 copy-done.3
  146.9 0.0 copy-done.4
  146.9 1.6 fusion.44
  148.5 0.0 copy-start.2
  148.5 0.1 broadcast_in_dim.2
  148.6 0.0 copy-done
  148.6 0.5 constant_dynamic-update-slice_fusion.3
  149.1 0.1 collective-permute-start
  149.2 1.7 collective-permute-start.1
  150.9 9.1 %collective-permute-done = bf16[256,768]{1,0:T(8,128)(2,1)} collective-permute-done((bf16[256,768]{1,0:T(8,128)(2,1)S(1)}, bf16[256,768]{1,0:T(8,128)(2,1)}, u32[]{:S(2)}, u32[]{:S(2)}) %collective-permute-start) | collective-permute-done | bytes 393248 | tf_op jit(solution)/shard_map/ppermute | solution.py:18
  160.0 0.0 collective-permute-start.2
  160.1 1.0 constant_dynamic-update-slice_fusion.2
  161.1 0.0 collective-permute-done.1
  161.1 1.0 constant_dynamic-update-slice_fusion.1
  162.1 5.4 %collective-permute-done.2 = bf16[256,768]{1,0:T(8,128)(2,1)} collective-permute-done((bf16[256,768]{1,0:T(8,128)(2,1)}, bf16[256,768]{1,0:T(8,128)(2,1)}, u32[]{:S(2)}, u32[]{:S(2)}) %collective-permute-start.2) | collective-permute-done | bytes 393248 | tf_op jit(solution)/shard_map/ppermute | solution.py:18
  167.6 1.0 constant_dynamic-update-slice_fusion
  168.6 0.0 copy-done.2
  168.6 38.8 %while.23 = (s32[]{:T(128)}, f32[8,128,768]{2,0,1:T(8,128)}, s32[2,16]{1,0:T(2,128)S(1)}, f32[2,16]{1,0:T(2,128)S(1)}, bf16[2,16,128,128]{3,2,1,0:T(8,128)(2,1)}...) while((s32[]{:T(128)}, f32[8,128,768]{2,0,1:T(8,128)}, ...), condition=%wide.region_4.5_spmd.clone, body=%wide.region_3.4_spmd.clone.sunk | while | flops 555222336 | bytes 28840704 | solution.py:104
  168.6 2.4 gather_fusion.1
  171.0 5.7 %fusion.86 = f32[16,128,768]{2,1,0:T(8,128)} fusion(bf16[16,128,768]{2,1,0:T(8,128)(2,1)} %gather_fusion.1, bf16[2,16,128,128]{3,2,1,0:T(8,128)(2,1)} %get-tuple-element.324, s32[]{:T(128)S(6)} %copy.40), kind=kOutput, calls=%fused_computation.32.clone.1 | convolution fusion | flops 402653184 | bytes 9961476 | tf_op jit(solution)/shard_map/while/body/eval_jaxpr/kpa,kpf->kaf/dot_general | solution.py:94
  176.8 11.0 %select_add_fusion.5 = f32[8,128,768]{2,0,1:T(8,128)} fusion(f32[8,128,768]{2,0,1:T(8,128)} %get-tuple-element.312, f32[16,128,768]{2,1,0:T(8,128)} %fusion.86, pred[]{:T(512)S(6)} %compare.10, f32[16]{0:T(128)S(1)} %fusion.87, s32[16]{0:T(128)S(1)} %fusion.88), kind=kOutput, calls=%fused_computation.31.clone.1 | convolution fusion | flops 152568064 | bytes 12583041 | tf_op jit(solution)/shard_map/while/body/eval_jaxpr/kc,kaf->caf/dot_general | solution.py:99
  187.8 2.4 gather_fusion.1
  190.2 5.7 %fusion.86 = f32[16,128,768]{2,1,0:T(8,128)} fusion(bf16[16,128,768]{2,1,0:T(8,128)(2,1)} %gather_fusion.1, bf16[2,16,128,128]{3,2,1,0:T(8,128)(2,1)} %get-tuple-element.324, s32[]{:T(128)S(6)} %copy.40), kind=kOutput, calls=%fused_computation.32.clone.1 | convolution fusion | flops 402653184 | bytes 9961476 | tf_op jit(solution)/shard_map/while/body/eval_jaxpr/kpa,kpf->kaf/dot_general | solution.py:94
  195.9 11.4 %select_add_fusion.5 = f32[8,128,768]{2,0,1:T(8,128)} fusion(f32[8,128,768]{2,0,1:T(8,128)} %get-tuple-element.312, f32[16,128,768]{2,1,0:T(8,128)} %fusion.86, pred[]{:T(512)S(6)} %compare.10, f32[16]{0:T(128)S(1)} %fusion.87, s32[16]{0:T(128)S(1)} %fusion.88), kind=kOutput, calls=%fused_computation.31.clone.1 | convolution fusion | flops 152568064 | bytes 12583041 | tf_op jit(solution)/shard_map/while/body/eval_jaxpr/kc,kaf->caf/dot_general | solution.py:99
  207.4 4.5 %copy.13 = f32[8,128,768]{2,1,0:T(8,128)} copy(f32[8,128,768]{2,0,1:T(8,128)} %get-tuple-element.92) | data formatting | bytes 6291456 | tf_op jit(solution)/shard_map/while | solution.py:104
  211.9 0.0 reduce-scatter.5.cloned.1.call-update
  211.9 74.4 %reduce-scatter.5.cloned.1.call-done = f32[128,768]{1,0:T(8,128)} async-done(((f32[1024,768]{1,0:T(8,128)}), f32[128,768]{1,0:T(8,128)}) %reduce-scatter.5.cloned.1.call-update) | async-done | bytes 393232 | tf_op jit(solution)/shard_map/reduce_scatter | solution.py:105
  286.3 1.7 convert_element_type.24
  (19 shorter events, 0.1 us)
Async XLA Ops:
  7.2 141.5 %copy-start = (bf16[768,768]{1,0:T(8,128)(2,1)S(1)}, bf16[768,768]{1,0:T(8,128)(2,1)}, u32[]{:S(2)}) copy-start(bf16[768,768]{1,0:T(8,128)(2,1)} %param.18) | copy-start | bytes 3538948
  7.2 49.9 %all-gather.2.cloned.1.call-start = ((), (), s32[]{:S(2)}) async-start(), calls=%async_computation.2 | async-start | bytes 1769472 | tf_op jit(solution)/shard_map/all_gather | solution.py:58
  7.9 139.0 %reduce-scatter.3.cloned.1.call-start = ((), (), s32[]{:S(2)}) async-start(), calls=%async_computation.3 | async-start | bytes 3932160 | tf_op jit(solution)/shard_map/reduce_scatter | solution.py:86
  57.1 3.3 %copy-start.5 = (bf16[2,768,768]{2,1,0:T(8,128)(2,1)S(1)}, bf16[2,768,768]{2,1,0:T(8,128)(2,1)}, u32[]{:S(2)}) copy-start(bf16[2,768,768]{2,1,0:T(8,128)(2,1)} %param.17) | copy-start | bytes 7077892
  57.1 3.3 %copy-start.6 = (bf16[1024,768]{1,0:T(8,128)(2,1)S(1)}, bf16[1024,768]{1,0:T(8,128)(2,1)}, u32[]{:S(2)}) copy-start(bf16[1024,768]{1,0:T(8,128)(2,1)} %all-gather.2.cloned.1.call-done) | copy-start | bytes 4718596
  61.8 2.0 copy-start.1
  110.5 36.4 %copy-start.3 = (bf16[768,768]{1,0:T(8,128)(2,1)S(1)}, bf16[768,768]{1,0:T(8,128)(2,1)}, u32[]{:S(2)}) copy-start(bf16[768,768]{1,0:T(8,128)(2,1)} %param.16) | copy-start | bytes 3538948
  110.5 36.4 %copy-start.4 = (bf16[256,768]{1,0:T(8,128)(2,1)S(1)}, bf16[256,768]{1,0:T(8,128)(2,1)}, u32[]{:S(2)}) copy-start(bf16[256,768]{1,0:T(8,128)(2,1)} %param.14) | copy-start | bytes 1179652
  110.5 175.8 %reduce-scatter.5.cloned.1.call-start = ((), (), s32[]{:S(2)}) async-start(), calls=%async_computation.4 | async-start | bytes 3538944 | tf_op jit(solution)/shard_map/reduce_scatter | solution.py:105
  148.5 20.1 %copy-start.2 = (bf16[256,768]{1,0:T(8,128)(2,1)}, bf16[256,768]{1,0:T(8,128)(2,1)S(1)}, u32[]{:S(2)}) copy-start(bf16[256,768]{1,0:T(8,128)(2,1)S(1)} %fusion.44) | copy-start | bytes 1179652
  149.1 10.9 %collective-permute-start = (bf16[256,768]{1,0:T(8,128)(2,1)S(1)}, bf16[256,768]{1,0:T(8,128)(2,1)}, u32[]{:S(2)}, u32[]{:S(2)}) collective-permute-start(bf16[256,768]{1,0:T(8,128)(2,1)S(1)} %get-tuple-element.179), channel_id=1, source_target_pairs={{0,1},{1,2},{2,3},{3,0},{4,5},{5,6},{6,7},{7,4},{8,9},{9,10},{10,1... | collective-permute-start | bytes 1179656 | tf_op jit(solution)/shard_map/ppermute | solution.py:18
  149.2 11.9 %collective-permute-start.1 = (bf16[256,768]{1,0:T(8,128)(2,1)S(1)}, bf16[256,768]{1,0:T(8,128)(2,1)}, u32[]{:S(2)}, u32[]{:S(2)}) collective-permute-start(bf16[256,768]{1,0:T(8,128)(2,1)S(1)} %get-tuple-element.179), channel_id=1, source_target_pairs={{0,3},{1,0},{2,1},{3,2},{4,7},{5,4},{6,5},{7,6},{8,11},{9,8},{10,9... | collective-permute-start | bytes 1179656 | tf_op jit(solution)/shard_map/ppermute | solution.py:23
  160.0 7.5 %collective-permute-start.2 = (bf16[256,768]{1,0:T(8,128)(2,1)}, bf16[256,768]{1,0:T(8,128)(2,1)}, u32[]{:S(2)}, u32[]{:S(2)}) collective-permute-start(bf16[256,768]{1,0:T(8,128)(2,1)} %collective-permute-done), channel_id=1, source_target_pairs={{0,1},{1,2},{2,3},{3,0},{4,5},{5,6},{6,7},{7,4},{8,9},{9,10},{10,1... | collective-permute-start | bytes 1179656 | tf_op jit(solution)/shard_map/ppermute | solution.py:18
Sparse Core Ops, SparseCore 0:
  10.2 46.8 all-gather.1
  110.6 36.2 reduce-scatter.2
  212.0 74.2 reduce-scatter.4
